TPU v7x, 32 devices: a whole 2x2x4 slice. The times are simulated.
32 devices in a mesh: ga: 8 (over z, x), band: 2 (over y), pool: 2 (over core).
Axes of the slice: x: 2, y: 2, z: 4, core: 2. Of those that a mesh axis runs over, the one named last changes fastest.
Arguments:
- psi_occ: bfloat16 [512, 64, 64, 128], P(('pool', 'band'), 'ga'), parts along dimension 0, may hold values from -9 to 9
- energies: float32 [32], P(('pool', 'band')), parts along dimension 0, may hold values from -0.8 to 0.6
- k_point: float32 [6], P('pool'), parts along dimension 0, may hold values from -0.5 to 0.5, as said below
- g_mask: int32 [128, 4096], P(('pool', 'ga')), parts along dimension 0, may hold values from 0 to 1, as said below
- v_local: float32 [64, 4096], P(None, 'ga'), may hold values from 1 to 4
- dv: float32 [3, 64, 4096], P(None, None, 'ga'), may hold values from -6 to 6
Outputs:
- response: float32 [32, 3, 64, 64, 128], P(('pool', 'band'), None, 'ga'), parts along dimension 0
- residual: float32 [32, 3, 64, 64, 128], P(('pool', 'band'), None, 'ga'), parts along dimension 0
There are 2 independent parts, one for each index of `pool`. A program takes and returns all parts, laid end to end along the dimension named above; an argument that names none is the same for every part. Nothing has to cross between parts.
Inputs may be any that keep to these rules, and one draw needn't show every extreme that they name: `k_point`: each component is a nonzero multiple of 0.25. `g_mask`: 1 exactly where the distance of (f(g1), f(g2), f(g3)) + k_point from the anchor is below 21, with f the signed frequency; so no 1 stands where |f(g2)| > 21 or |f(g3)| > 21, and in every draw some 1 stands where |f(g2)| = 21.
All inputs are finite; a program needn't handle non-finite values.
Results may differ from a plain program's by a relative error of at most 0.0044.
Values may be sent and summed in bfloat16 or wider, within the bound.
No kernel may reach another device: no remote copies, remote signals or barrier semaphores. Data moves between devices by JAX's collectives and lax.ppermute only.
A program may use at most 192 MiB of HBM per device.

v0:
```python
import math

import jax
import jax.numpy as jnp
from jax import lax
from jax.sharding import PartitionSpec as P

BOX = 64
GCUT = 21
NPERT = 3
ITERS = 2
STRIDE = 16


cell_length = 16.5
shift_weight = 8.0


def quarter_turn(values):
    halfway = values.shape[-1] // 2
    return jnp.concatenate([-values[..., halfway:], values[..., :halfway]], axis=-1)


def minus_turn(values):
    halfway = values.shape[-1] // 2
    return jnp.concatenate([values[..., halfway:], -values[..., :halfway]], axis=-1)


def phase_tables(length, phase_sign):
    indices = jnp.arange(length, dtype=jnp.int32)
    product = indices[:, None] * indices[None, :] % length
    angle = product.astype(jnp.float32) * (2.0 * math.pi / length)
    return (jnp.cos(angle), phase_sign * jnp.sin(angle))


def transform_rows(values, which, phase_sign):
    cosine_table, sine_table = phase_tables(values.shape[which], phase_sign)
    form = "ab,sbyz->sayz" if which == 1 else "ab,sxbz->sxaz"
    first = jnp.einsum(form, cosine_table, values, precision=lax.Precision.HIGHEST)
    second = jnp.einsum(form, sine_table, values, precision=lax.Precision.HIGHEST)
    return first + quarter_turn(second)


def transform_last(values, phase_sign):
    cosine_table, sine_table = phase_tables(values.shape[-1] // 2, phase_sign)
    upper = jnp.concatenate([cosine_table, sine_table], axis=1)
    lower = jnp.concatenate([-sine_table, cosine_table], axis=1)
    matrix = jnp.concatenate([upper, lower], axis=0)
    return jnp.dot(values, matrix, precision=lax.Precision.HIGHEST)


def keep_rows(values):
    return jnp.concatenate([values[:, :, : GCUT + 1], values[:, :, BOX - GCUT :]], axis=2)


def restore_rows(values):
    filler = jnp.zeros(
        (values.shape[0], values.shape[1], BOX - 2 * GCUT - 1, values.shape[3]), values.dtype
    )
    return jnp.concatenate([values[:, :, : GCUT + 1], filler, values[:, :, GCUT + 1 :]], axis=2)


def local_inner(first, second):
    return jnp.sum(first * second, axis=(1, 2, 3)) / BOX**3


def global_norms(values):
    return lax.psum(local_inner(values, values), "ga")


def on_device(psi_occ, energies, k_point, g_mask, v_local, dv):
    slab_rows = psi_occ.shape[1]
    row_count = v_local.shape[1] // BOX
    ga_index = lax.axis_index("ga")
    indices = jnp.arange(BOX, dtype=jnp.int32)
    signed = jnp.where(indices < BOX // 2, indices, indices - BOX).astype(jnp.float32)
    owned = ga_index * slab_rows + jnp.arange(slab_rows, dtype=jnp.int32)
    freq_first = jnp.where(owned < BOX // 2, owned, owned - BOX).astype(jnp.float32)
    factor = 0.5 * (2.0 * math.pi / cell_length) ** 2
    kinetic = factor * (
        (freq_first[:, None, None] + k_point[0]) ** 2
        + (signed[None, :, None] + k_point[1]) ** 2
        + (signed[None, None, :] + k_point[2]) ** 2
    )
    kinetic = jnp.concatenate([kinetic, kinetic], axis=-1)
    sphere = g_mask.reshape(slab_rows, BOX, BOX).astype(jnp.float32)
    sphere = jnp.concatenate([sphere, sphere], axis=-1)
    occupied = psi_occ * sphere.astype(jnp.bfloat16)
    solved = occupied[::STRIDE].astype(jnp.float32)
    energy_shift = jnp.repeat(energies, NPERT)[:, None, None, None]
    potential = v_local.reshape(BOX, row_count, BOX)
    potential = jnp.concatenate([potential, potential], axis=-1)
    changes = dv.reshape(NPERT, BOX, row_count, BOX)
    changes = jnp.concatenate([changes, changes], axis=-1)
    occupied_all = lax.all_gather(keep_rows(occupied), "band", axis=0, tiled=True)
    row_kept = 2 * GCUT + 1
    flat_panel = occupied_all.reshape(occupied_all.shape[0], -1)

    def project_occupied(values):
        count = values.shape[0]
        part = keep_rows(values)
        lowered = part.astype(jnp.bfloat16)
        stacked = jnp.concatenate([lowered, minus_turn(lowered)], axis=0).reshape(2 * count, -1)
        partial_value = lax.dot_general(
            flat_panel, stacked, (((1,), (1,)), ((), ())), preferred_element_type=jnp.float32
        )
        correlation = lax.psum(partial_value, "ga")
        low_correlation = correlation.astype(jnp.bfloat16)
        product = lax.dot_general(
            low_correlation,
            flat_panel,
            (((0,), (0,)), ((), ())),
            preferred_element_type=jnp.float32,
        )
        product = product.reshape(2 * count, slab_rows, row_kept, 2 * BOX)
        result = product[:count] + quarter_turn(product[count:])
        result = restore_rows(result)
        return result / BOX**3

    def through_grid(coeffs, on_grid):
        near = transform_rows(transform_last(coeffs, 1.0), 2, 1.0)
        grid_values = transform_rows(
            lax.all_to_all(near, "ga", split_axis=2, concat_axis=1, tiled=True), 1, 1.0
        )
        result = on_grid(grid_values)
        back = transform_rows(result, 1, -1.0)
        moved = lax.all_to_all(back, "ga", split_axis=1, concat_axis=2, tiled=True)
        far = transform_last(transform_rows(moved, 2, -1.0), -1.0)
        return far * (sphere / BOX**3)

    def with_changes(grid_values):
        spread = grid_values[:, None] * changes[None]
        return spread.reshape(-1, BOX, row_count, 2 * BOX)

    def with_potential(grid_values):
        return grid_values * potential

    source = through_grid(solved, with_changes)
    right_side = project_occupied(source) - source
    response = jnp.zeros_like(right_side)
    residual = right_side
    direction = right_side
    norm_now = global_norms(residual)
    for iteration in range(ITERS):
        image = (
            (kinetic - energy_shift) * direction
            + through_grid(direction, with_potential)
            + shift_weight * project_occupied(direction)
        )
        step_size = norm_now / lax.psum(local_inner(direction, image), "ga")
        response = response + step_size[:, None, None, None] * direction
        residual = residual - step_size[:, None, None, None] * image
        if iteration + 1 < ITERS:
            fresh = global_norms(residual)
            direction = residual + (fresh / norm_now)[:, None, None, None] * direction
            norm_now = fresh
    local_bands = energies.shape[0]
    response = response.reshape(local_bands, NPERT, slab_rows, BOX, 2 * BOX)
    residual = residual.reshape(local_bands, NPERT, slab_rows, BOX, 2 * BOX)
    return (response, residual)


def solution(mesh):
    placed = (
        P(("pool", "band"), "ga", None, None),
        P(("pool", "band")),
        P("pool"),
        P(("pool", "ga"), None),
        P(None, "ga"),
        P(None, None, "ga"),
    )
    return jax.shard_map(
        on_device,
        mesh=mesh,
        in_specs=placed,
        out_specs=(
            P(("pool", "band"), None, "ga", None, None),
            P(("pool", "band"), None, "ga", None, None),
        ),
        check_vma=False,
    )
```

profile of v0, /device:TPU:0, one launch (start us, length us, event | category | flops | bytes accessed | tf_op | source)
XLA Modules:
  0.0 1453.6 jit_solution(15352902377339684650)
XLA Ops:
  63.2 46.6 %all-to-all-done = f32[8,8,64,128]{3,1,0,2:T(8,128)S(1)} async-done(((f32[8,8,64,128]{3,1,0,2:T(8,128)}), f32[8,8,64,128]{3,1,0,2:T(8,128)S(1)}, u32[]{:S(2)}, u32[]{:S(2)}) %all-to-all-start) | async-done | bytes 2097184 | tf_op jit(solution)/shard_map/all_to_all | solution.py:123
  135.3 11.9 maximum_add_fusion
  159.6 136.3 %all-to-all-done.1 = f32[24,64,8,128]{3,2,0,1:T(8,128)} async-done(((f32[24,64,8,128]{3,2,0,1:T(8,128)}), f32[24,64,8,128]{3,2,0,1:T(8,128)}, u32[]{:S(2)}, u32[]{:S(2)}) %all-to-all-start.1) | async-done | bytes 6291488 | tf_op jit(solution)/shard_map/all_to_all | solution.py:127
  320.8 11.7 multiply_convert_fusion
  340.0 31.8 %copy.35 = bf16[256,8,43,128]{0,3,2,1:T(8,128)(2,1)} copy(bf16[256,8,43,128]{3,1,2,0:T(8,128)(2,1)} %all-gather.2.cloned.1.call-done) | data formatting | bytes 45088768 | tf_op jit(solution)/shard_map/all_gather | solution.py:95
  371.8 11.7 fusion.88
  383.6 35.7 %psum.49 = bf16[256,48]{0,1:T(8,128)(2,1)S(1)} all-reduce(f32[256,48]{0,1:T(8,128)S(1)} %fusion.88), channel_id=1, replica_groups=mesh['ga'=8,'band'=2,'pool'=2] {'ga'}, use_global_device_ids=true, to_apply=%region_0.1 | all-reduce | flops 12288 | bytes 73728 | tf_op jit(solution)/shard_map/psum | solution.py:107
  419.3 12.9 fusion.292
  492.4 11.7 maximum_add_fusion.3
  541.5 128.9 %psum.51 = bf16[256,48]{0,1:T(8,128)(2,1)S(1)} all-reduce(f32[256,48]{0,1:T(8,128)S(1)} %fusion.91), channel_id=1, replica_groups=mesh['ga'=8,'band'=2,'pool'=2] {'ga'}, use_global_device_ids=true, to_apply=%region_3.4 | all-reduce | flops 12288 | bytes 73728 | tf_op jit(solution)/shard_map/psum | solution.py:107
  712.7 12.8 maximum_add_fusion.5
  736.6 12.9 fusion.291
  782.7 85.7 %all-to-all-done.3 = f32[24,64,8,128]{3,2,0,1:T(8,128)} async-done(((f32[24,64,8,128]{3,2,0,1:T(8,128)}), f32[24,64,8,128]{3,2,0,1:T(8,128)}, u32[]{:S(2)}, u32[]{:S(2)}) %all-to-all-start.3) | async-done | bytes 6291488 | tf_op jit(solution)/shard_map/all_to_all | solution.py:127
  899.2 14.3 multiply_reduce_fusion.2
  913.5 19.5 %all-reduce = (f32[24]{0:T(128)S(1)}, f32[24]{0:T(128)S(1)}) all-reduce(f32[24]{0:T(128)S(1)} %broadcast_multiply_fusion.12, f32[24]{0:T(128)S(1)} %broadcast_multiply_fusion.11), channel_id=1, replica_groups=mesh['ga'=8,'band'=2,'pool'=2] {'ga'}, use_global_device_ids=true, to_apply=%region_2.3 | all-reduce | flops 48 | bytes 384 | tf_op jit(solution)/shard_map/psum | solution.py:68
  942.5 17.3 %psum.53 = f32[24]{0:T(128)S(1)} all-reduce(f32[24]{0:T(128)S(1)} %broadcast_multiply_fusion.10), channel_id=1, replica_groups=mesh['ga'=8,'band'=2,'pool'=2] {'ga'}, use_global_device_ids=true, to_apply=%region_7.8 | all-reduce | flops 24 | bytes 192 | tf_op jit(solution)/shard_map/psum | solution.py:68
  993.1 11.5 maximum_add_fusion.8
  1032.9 137.9 %psum.54 = bf16[256,48]{0,1:T(8,128)(2,1)S(1)} all-reduce(f32[256,48]{0,1:T(8,128)S(1)} %fusion.94), channel_id=1, replica_groups=mesh['ga'=8,'band'=2,'pool'=2] {'ga'}, use_global_device_ids=true, to_apply=%region_8.9 | all-reduce | flops 12288 | bytes 73728 | tf_op jit(solution)/shard_map/psum | solution.py:107
  1213.3 12.6 maximum_add_fusion.10
  1236.8 13.0 fusion.290
  1283.1 85.5 %all-to-all-done.5 = f32[24,64,8,128]{3,2,0,1:T(8,128)} async-done(((f32[24,64,8,128]{3,2,0,1:T(8,128)}), f32[24,64,8,128]{3,2,0,1:T(8,128)}, u32[]{:S(2)}, u32[]{:S(2)}) %all-to-all-start.5) | async-done | bytes 6291488 | tf_op jit(solution)/shard_map/all_to_all | solution.py:127
  1399.5 13.8 multiply_reduce_fusion
  1413.3 19.4 %psum.55 = f32[24]{0:T(128)S(1)} all-reduce(f32[24]{0:T(128)S(1)} %broadcast_multiply_fusion.9), channel_id=1, replica_groups=mesh['ga'=8,'band'=2,'pool'=2] {'ga'}, use_global_device_ids=true, to_apply=%region_10.11 | all-reduce | flops 24 | bytes 192 | tf_op jit(solution)/shard_map/psum | solution.py:150
  1432.8 13.8 multiply_subtract_fusion
  (196 shorter events, 529.4 us)
Async XLA Ops:
  7.2 332.9 %all-gather.2.cloned.1.call-start = ((), (), s32[]{:S(2)}) async-start(), calls=%async_computation.6 | async-start | bytes 33816576 | tf_op jit(solution)/shard_map/all_gather | solution.py:95
  17.1 19.9 %copy-start.4 = (bf16[128,8,64,128]{3,2,1,0:T(8,128)(2,1)}, bf16[128,8,64,128]{3,2,1,0:T(8,128)(2,1)S(1)}, u32[]{:S(2)}) copy-start(bf16[128,8,64,128]{3,2,1,0:T(8,128)(2,1)S(1)} %broadcast_multiply_fusion) | copy-start | bytes 50331652
  43.1 425.1 %copy-start.10 = (f32[64,64]{1,0:T(8,128)}, f32[64,64]{1,0:T(8,128)S(1)}, u32[]{:S(2)}) copy-start(f32[64,64]{1,0:T(8,128)S(1)} %get-tuple-element.64) | copy-start | bytes 49156
  43.3 424.9 %copy-start.12 = (f32[64,64]{1,0:T(8,128)}, f32[64,64]{1,0:T(8,128)S(1)}, u32[]{:S(2)}) copy-start(f32[64,64]{1,0:T(8,128)S(1)} %fusion.161) | copy-start | bytes 49156
  51.3 10.4 copy-start.17
  53.9 55.9 %all-to-all-start = ((f32[8,8,64,128]{3,1,0,2:T(8,128)}), f32[8,8,64,128]{3,1,0,2:T(8,128)S(1)}, u32[]{:S(2)}, u32[]{:S(2)}) async-start(f32[8,8,64,128]{3,1,0,2:T(8,128)} %copy.28), calls=%async_computation | async-start | bytes 4194304 | tf_op jit(solution)/shard_map/all_to_all | solution.py:123
  153.5 142.4 %all-to-all-start.1 = ((f32[24,64,8,128]{3,2,0,1:T(8,128)}), f32[24,64,8,128]{3,2,0,1:T(8,128)}, u32[]{:S(2)}, u32[]{:S(2)}) async-start(f32[24,64,8,128]{3,2,0,1:T(8,128)} %copy.31), calls=%async_computation.1 | async-start | bytes 12582912 | tf_op jit(solution)/shard_map/all_to_all | solution.py:127
  159.4 161.3 %copy-start.14 = (f32[64,64]{1,0:T(8,128)}, f32[64,64]{1,0:T(8,128)S(1)}, u32[]{:S(2)}) copy-start(f32[64,64]{1,0:T(8,128)S(1)} %get-tuple-element.66) | copy-start | bytes 49156
  445.1 14.3 slice-start.6
  450.6 14.6 %slice-start.4 = ((s8[6291456]{0:T(1024)(128)(4,1)}), s8[4194304]{0:T(1024)(128)(4,1)S(1)}, s32[]{:S(2)}) async-start(s8[6291456]{0:T(1024)(128)(4,1)} %bitcast.259), calls=%async_computation.11 | async-start | bytes 8388608
  510.4 8.9 copy-start.18
  510.4 14.2 copy-start.6
  510.4 160.0 %all-to-all-start.2 = ((f32[24,8,64,128]{3,1,0,2:T(8,128)}), f32[24,8,64,128]{3,1,0,2:T(8,128)}, u32[]{:S(2)}, u32[]{:S(2)}) async-start(f32[24,8,64,128]{3,1,0,2:T(8,128)} %copy.36), calls=%async_computation.2 | async-start | bytes 12582912 | tf_op jit(solution)/shard_map/all_to_all | solution.py:123
  731.9 136.5 %all-to-all-start.3 = ((f32[24,64,8,128]{3,2,0,1:T(8,128)}), f32[24,64,8,128]{3,2,0,1:T(8,128)}, u32[]{:S(2)}, u32[]{:S(2)}) async-start(f32[24,64,8,128]{3,2,0,1:T(8,128)} %copy.40), calls=%async_computation.3 | async-start | bytes 12582912 | tf_op jit(solution)/shard_map/all_to_all | solution.py:127
  762.3 13.2 slice-start.8
  878.1 21.1 %slice-start = ((s8[6291456]{0:T(1024)(128)(4,1)}), s8[4194304]{0:T(1024)(128)(4,1)S(1)}, s32[]{:S(2)}) async-start(s8[6291456]{0:T(1024)(128)(4,1)} %bitcast.253), calls=%async_computation.7 | async-start | bytes 8388608
  888.0 11.2 slice-start.1
  888.0 11.2 copy-start.15
  888.0 11.2 copy-start.16
  1010.9 160.0 %all-to-all-start.4 = ((f32[24,8,64,128]{3,1,0,2:T(8,128)}), f32[24,8,64,128]{3,1,0,2:T(8,128)}, u32[]{:S(2)}, u32[]{:S(2)}) async-start(f32[24,8,64,128]{3,1,0,2:T(8,128)} %copy.44), calls=%async_computation.4 | async-start | bytes 12582912 | tf_op jit(solution)/shard_map/all_to_all | solution.py:123
  1232.1 136.5 %all-to-all-start.5 = ((f32[24,64,8,128]{3,2,0,1:T(8,128)}), f32[24,64,8,128]{3,2,0,1:T(8,128)}, u32[]{:S(2)}, u32[]{:S(2)}) async-start(f32[24,64,8,128]{3,2,0,1:T(8,128)} %copy.46), calls=%async_computation.5 | async-start | bytes 12582912 | tf_op jit(solution)/shard_map/all_to_all | solution.py:127
  1262.6 13.3 slice-start.10
  1378.4 21.1 %slice-start.2 = ((s8[6291456]{0:T(1024)(128)(4,1)}), s8[4194304]{0:T(1024)(128)(4,1)S(1)}, s32[]{:S(2)}) async-start(s8[6291456]{0:T(1024)(128)(4,1)} %bitcast.255), calls=%async_computation.9 | async-start | bytes 8388608
  1388.3 11.2 slice-start.3
  (15 other events, 83.4 us)
Sparse Core Ops, SparseCore 0:
  43.1 267.3 all-gather.1
where the time goes:
time: 1460 us; the launch traced here: 1450 us
  blocking collectives  359 us (25%)
  waiting for transfers between devices  354 us (24%)
  matrix products  328 us (22%)
  other arithmetic  205 us (14%)
  local copies, waits for them, and re-layouts  160 us (11%)
  starting transfers between devices  32.9 us (2%)
  between operations  15 us (1%)
    all_to_all x3, waiting for transfers between devices, through_grid(): moved = lax.all_to_all(back, 'ga', split_axis=1, concat_axis=2, tiled=True)  307 us
    psum x3, blocking collectives, project_occupied(): correlation = lax.psum(partial_value, 'ga')  302 us
    dot_general x12, matrix products, transform_rows(): jnp.einsum(form, cosine_table, values, precision=lax.Precision.HIGHEST)  118 us
    neg x15, other arithmetic, quarter_turn(): -values[..., halfway:]  116 us
    dot_general x12, matrix products, transform_rows(): jnp.einsum(form, sine_table, values, precision=lax.Precision.HIGHEST)  85.6 us
    slice x9, local copies, waits for them, and re-layouts, project_occupied(): result = product[:count] + quarter_turn(product[count:])  55 us
    dot_general x6, matrix products, transform_last(): return jnp.dot(values, matrix, precision=lax.Precision.HIGHEST)  52.6 us
    all_to_all x3, waiting for transfers between devices, through_grid(): lax.all_to_all(near, 'ga', split_axis=2, concat_axis=1, tiled=True)  46.7 us
  transfers between devices with their start and end apart: 7, of which 4 were waited for; matrix products, arithmetic and copies ran while one was open for 16% of the time, Pallas kernels for 0%

commit v1 on v0

v1 whole, which is shorter than its diff:
```python
import math

import jax
import jax.numpy as jnp
import numpy as np
from jax import lax
from jax.experimental import pallas as pl
from jax.experimental.pallas import tpu as pltpu
from jax.sharding import PartitionSpec as P

BOX = 64
GCUT = 21
KEPT = 2 * GCUT + 1
PADDED = 48
NPERT = 3
ITERS = 2
STRIDE = 16
MIDDLE = 2.5


cell_length = 16.5
shift_weight = 8.0


def quarter_turn(values):
    halfway = values.shape[-1] // 2
    return jnp.concatenate([-values[..., halfway:], values[..., :halfway]], axis=-1)


def minus_turn(values):
    halfway = values.shape[-1] // 2
    return jnp.concatenate([values[..., halfway:], -values[..., :halfway]], axis=-1)


def phase_tables(phase_sign):
    indices = np.arange(BOX)
    angle = (indices[:, None] * indices[None, :] % BOX) * (2.0 * math.pi / BOX)
    return np.cos(angle), phase_sign * np.sin(angle)


def kept_positions():
    return np.concatenate([np.arange(GCUT + 1), np.arange(BOX - GCUT, BOX)])


def split_table(table):
    table = np.asarray(table, np.float32)
    high = table.astype(jnp.bfloat16)
    low = (table - high.astype(np.float32)).astype(jnp.bfloat16)
    return np.stack([high, low])


def transform_tables():
    keep = kept_positions()
    tables = []
    for sign in (1.0, -1.0):
        cosine, sine = phase_tables(sign)
        lanes = np.block([[cosine, sine], [-sine, cosine]])
        first = np.concatenate([cosine, sine], axis=1)
        if sign > 0:
            second = np.zeros((BOX, 2 * PADDED))
            second[:, :KEPT] = cosine[:, keep]
            second[:, PADDED : PADDED + KEPT] = sine[:, keep]
        else:
            second = np.zeros((PADDED, 2 * BOX))
            second[:KEPT, :BOX] = cosine[keep]
            second[:KEPT, BOX:] = sine[keep]
        tables += [split_table(lanes), split_table(first), split_table(second)]
    return tables


def keep_rows(values, axis):
    lead = lax.slice_in_dim(values, 0, GCUT + 1, axis=axis)
    tail = lax.slice_in_dim(values, BOX - GCUT, BOX, axis=axis)
    return jnp.concatenate([lead, tail], axis=axis)


def grid_kernel(exact, x_ref, w_ref, li_ref, fi_ref, si_ref, lf_ref, ff_ref, sf_ref, o_ref, u_ref, t_ref, r_ref, q_ref):
    lane = lax.broadcasted_iota(jnp.int32, (1, 2 * BOX), 1)
    sign = jnp.where(lane < BOX, -1.0, 1.0).astype(jnp.float32)

    def plain(left, right):
        return jnp.dot(left, right, preferred_element_type=jnp.float32)

    def halves(values):
        high = values.astype(jnp.bfloat16)
        if not exact:
            return high, None
        return high, (values - high.astype(jnp.float32)).astype(jnp.bfloat16)

    def from_left(table_ref, values):
        turned = pltpu.roll(values, BOX, 1) * sign
        high, low = halves(jnp.concatenate([values, turned], axis=0))
        total = plain(table_ref[0], high)
        if exact:
            total = total + (plain(table_ref[1], high) + plain(table_ref[0], low))
        return total

    def from_right(values, table_ref):
        high, low = halves(values)
        total = plain(high, table_ref[0])
        if exact:
            total = total + (plain(high, table_ref[1]) + plain(low, table_ref[0]))
        return total

    @pl.when(pl.program_id(1) == 0)
    def _():
        t_ref[KEPT:] = jnp.zeros((PADDED - KEPT, BOX, 2 * BOX), jnp.float32)
        rows = x_ref[0].reshape(KEPT * BOX, 2 * BOX).astype(jnp.float32)
        u_ref[...] = from_right(rows, li_ref).reshape(KEPT, BOX, 2 * BOX)
        for b in range(KEPT):
            t_ref[b] = from_left(fi_ref, u_ref[b])
        for a in range(BOX):
            r_ref[a] = from_left(si_ref, t_ref[:, a, :])

    for a in range(BOX):
        q_ref[a] = from_left(sf_ref, r_ref[a] * w_ref[0, a])
    q_ref[...] = from_right(q_ref[...].reshape(BOX * PADDED, 2 * BOX), lf_ref).reshape(BOX, PADDED, 2 * BOX)
    for b in range(KEPT):
        o_ref[0, b] = from_left(ff_ref, q_ref[:, b, :]).astype(o_ref.dtype)


def apply_fields(coeffs, fields, tables, exact, out_type):
    count, spread = coeffs.shape[0], fields.shape[0]
    whole = lambda array: pl.BlockSpec(array.shape, lambda i, j: (0,) * array.ndim)
    return pl.pallas_call(
        lambda *refs: grid_kernel(exact, *refs),
        grid=(count, spread),
        in_specs=[
            pl.BlockSpec((1, KEPT, BOX, 2 * BOX), lambda i, j: (i, 0, 0, 0)),
            pl.BlockSpec((1, BOX, BOX, 2 * BOX), lambda i, j: (j, 0, 0, 0)),
        ]
        + [whole(table) for table in tables],
        out_specs=pl.BlockSpec((1, KEPT, BOX, 2 * BOX), lambda i, j: (i * spread + j, 0, 0, 0)),
        out_shape=jax.ShapeDtypeStruct((count * spread, KEPT, BOX, 2 * BOX), out_type),
        scratch_shapes=[
            pltpu.VMEM((KEPT, BOX, 2 * BOX), jnp.float32),
            pltpu.VMEM((PADDED, BOX, 2 * BOX), jnp.float32),
            pltpu.VMEM((BOX, BOX, 2 * BOX), jnp.float32),
            pltpu.VMEM((BOX, PADDED, 2 * BOX), jnp.float32),
        ],
        compiler_params=pltpu.CompilerParams(
            dimension_semantics=("arbitrary", "arbitrary"), vmem_limit_bytes=50 * 2**20
        ),
        name="grid_exact" if exact else "grid_apply",
    )(coeffs, fields, *tables)


def on_device(psi_occ, energies, k_point, g_mask, v_local, dv):
    slab_rows = psi_occ.shape[1]
    row_count = v_local.shape[1] // BOX
    ga_index = lax.axis_index("ga")
    signed = np.where(np.arange(BOX) < BOX // 2, np.arange(BOX), np.arange(BOX) - BOX).astype(np.float32)
    second_freq = jnp.asarray(signed[kept_positions()])
    signed = jnp.asarray(signed)
    owned = ga_index * slab_rows + jnp.arange(slab_rows, dtype=jnp.int32)
    freq_first = jnp.where(owned < BOX // 2, owned, owned - BOX).astype(jnp.float32)
    factor = 0.5 * (2.0 * math.pi / cell_length) ** 2
    kinetic = factor * (
        (freq_first[None, :, None] + k_point[0]) ** 2
        + (second_freq[:, None, None] + k_point[1]) ** 2
        + (signed[None, None, :] + k_point[2]) ** 2
    )
    kinetic = jnp.concatenate([kinetic, kinetic], axis=-1)
    sphere = keep_rows(g_mask.reshape(slab_rows, BOX, BOX), 1).transpose(1, 0, 2).astype(jnp.float32)
    sphere = jnp.concatenate([sphere, sphere], axis=-1)
    tables = [jnp.asarray(table) for table in transform_tables()]

    local_bands = energies.shape[0]

    def to_boxes(values):
        short = -values.shape[0] % lax.axis_size("ga")
        if short:
            values = jnp.concatenate([values, jnp.zeros((short,) + values.shape[1:], values.dtype)], axis=0)
        return lax.all_to_all(values, "ga", split_axis=0, concat_axis=2, tiled=True)

    low_sphere = sphere.astype(jnp.bfloat16)
    solved = keep_rows(psi_occ[::STRIDE], 2).transpose(0, 2, 1, 3) * low_sphere
    moved_solved = to_boxes(solved)

    fields = jnp.concatenate([dv, v_local[None] - MIDDLE], axis=0) / BOX**3
    fields = lax.all_gather(fields, "ga", axis=0)
    fields = fields.reshape(-1, NPERT + 1, BOX, row_count, BOX).transpose(1, 2, 0, 3, 4)
    fields = fields.reshape(NPERT + 1, BOX, BOX, BOX)
    fields = jnp.concatenate([fields, fields], axis=-1)
    changes, potential = fields[:NPERT], fields[NPERT:]

    occupied = keep_rows(psi_occ, 2).transpose(0, 2, 1, 3) * low_sphere
    flat_panel = lax.all_gather(
        occupied.reshape(occupied.shape[0], -1), "band", axis=0, tiled=True
    )
    energy_shift = jnp.repeat(energies, NPERT)[:, None, None, None]

    def project_occupied(values):
        count = values.shape[0]
        lowered = values.astype(jnp.bfloat16)
        stacked = jnp.concatenate([lowered, minus_turn(lowered)], axis=0).reshape(2 * count, -1)
        partial_value = lax.dot_general(
            flat_panel, stacked, (((1,), (1,)), ((), ())), preferred_element_type=jnp.float32
        )
        correlation = lax.psum(partial_value, "ga")
        low_correlation = correlation.astype(jnp.bfloat16)
        product = lax.dot_general(
            low_correlation,
            flat_panel,
            (((0,), (0,)), ((), ())),
            preferred_element_type=jnp.float32,
        )
        product = product.reshape(2 * count, KEPT, slab_rows, 2 * BOX)
        return (product[:count] + quarter_turn(product[count:])) / BOX**3

    def back_to_slabs(values):
        slabs = lax.all_to_all(values, "ga", split_axis=2, concat_axis=0, tiled=True)
        return slabs[: local_bands * NPERT].astype(jnp.float32) * sphere

    def local_inner(first, second):
        return jnp.sum(first * second, axis=(1, 2, 3)) / BOX**3

    diagonal = kinetic + MIDDLE - energy_shift

    def operator(direction):
        moved = to_boxes(direction.astype(jnp.bfloat16))
        applied = back_to_slabs(apply_fields(moved, potential, tables, False, jnp.bfloat16))
        return diagonal * direction + applied + shift_weight * project_occupied(direction)

    source = back_to_slabs(apply_fields(moved_solved, changes, tables, True, jnp.float32))
    right_side = project_occupied(source) - source
    residual = right_side
    direction = right_side
    response = None
    norm_now = None
    for iteration in range(ITERS):
        image = operator(direction)
        sums = [local_inner(direction, image)]
        if iteration == 0:
            sums.append(local_inner(residual, residual))
        if iteration + 1 < ITERS:
            sums += [local_inner(residual, image), local_inner(image, image)]
        sums = lax.psum(jnp.stack(sums), "ga")
        if iteration == 0:
            norm_now = sums[1]
        step_size = norm_now / sums[0]
        step = step_size[:, None, None, None]
        response = step * direction if response is None else response + step * direction
        residual = residual - step * image
        if iteration + 1 < ITERS:
            fresh = norm_now - 2.0 * step_size * sums[-2] + step_size**2 * sums[-1]
            direction = residual + (fresh / norm_now)[:, None, None, None] * direction
            norm_now = fresh

    def restore(values):
        values = values.transpose(0, 2, 1, 3)
        filler = jnp.zeros(values.shape[:2] + (BOX - KEPT, 2 * BOX), values.dtype)
        values = jnp.concatenate([values[:, :, : GCUT + 1], filler, values[:, :, GCUT + 1 :]], axis=2)
        return values.reshape(local_bands, NPERT, slab_rows, BOX, 2 * BOX)

    return (restore(response), restore(residual))


def solution(mesh):
    placed = (
        P(("pool", "band"), "ga", None, None),
        P(("pool", "band")),
        P("pool"),
        P(("pool", "ga"), None),
        P(None, "ga"),
        P(None, None, "ga"),
    )
    return jax.shard_map(
        on_device,
        mesh=mesh,
        in_specs=placed,
        out_specs=(
            P(("pool", "band"), None, "ga", None, None),
            P(("pool", "band"), None, "ga", None, None),
        ),
        check_vma=False,
    )
```

time: 1460 us -> 923 us (0.63)
  matrix products: 328 us -> 76.8 us
  blocking collectives: 359 us -> 241 us
  waiting for transfers between devices: 354 us -> 240 us
  other arithmetic: 205 us -> 119 us
  Pallas kernels: 0 us -> 51.4 us
    dot_general x30 -> x0, matrix products: 256 us -> none  [the longest x12 118 us: transform_rows(): jnp.einsum(form, cosine_table, values, precision=lax.Precision.HIGHEST)]
    all_to_all x6 -> x5, waiting for transfers between devices: 354 us -> 157 us  [the longest x3 97.7 us: back_to_slabs(): lax.all_to_all(values, 'ga', split_axis=2, concat_axis=0, tiled=True)]
    psum x3, blocking collectives: 302 us -> 162 us  [project_occupied(): correlation = lax.psum(partial_value, 'ga')]
    neg x15 -> x3, other arithmetic: 116 us -> 7.4 us  [quarter_turn(): -values[..., halfway:]]
    all_gather x1 -> x2, waiting for transfers between devices: 0.01 us -> 82.7 us  [the longest x1 82.5 us: on_device(): lax.all_gather(occupied.reshape(occupied.shape[0], -1), 'band', axis=0, t...]
    unnamed x64, local copies, waits for them, and re-layouts: 6.15 us -> 66.8 us
    slice x23 -> x11, local copies, waits for them, and re-layouts: 76.5 us -> 18.5 us  [the longest x3 9.56 us: keep_rows(): tail = lax.slice_in_dim(values, BOX - GCUT, BOX, axis=axis)]
    pallas_call x0 -> x3, Pallas kernels: none -> 51.4 us  [apply_fields(): pl.pallas_call(lambda *refs: grid_kernel(exact, *refs), grid=(count, spre...]
  transfers between devices with their start and end apart: 7 -> 7, of which waited for: 4 -> 5; matrix products, arithmetic and copies ran while one was open for 16% -> 21% of each run, Pallas kernels for 0% -> 3%
where the time goes in v1:
time: 923 us; the launch traced here: 916 us
  blocking collectives  241 us (26%)
  waiting for transfers between devices  240 us (26%)
  local copies, waits for them, and re-layouts  152 us (16%)
  other arithmetic  119 us (13%)
  matrix products  76.8 us (8%)
  Pallas kernels  51.4 us (6%)
  starting transfers between devices  22.2 us (2%)
  between operations  14.8 us (2%)
    psum x3, blocking collectives, project_occupied(): correlation = lax.psum(partial_value, 'ga')  162 us
    all_to_all x3, waiting for transfers between devices, back_to_slabs(): lax.all_to_all(values, 'ga', split_axis=2, concat_axis=0, tiled=True)  97.7 us
    all_gather x1, waiting for transfers between devices, on_device(): lax.all_gather(occupied.reshape(occupied.shape[0], -1), 'band', axis=0, t...  82.5 us
    unnamed x64, local copies, waits for them, and re-layouts  66.8 us
    all_to_all x2, waiting for transfers between devices, to_boxes(): return lax.all_to_all(values, 'ga', split_axis=0, concat_axis=2, tiled=True)  59.2 us
    pallas_call x3, Pallas kernels, apply_fields(): pl.pallas_call(lambda *refs: grid_kernel(exact, *refs), grid=(count, spre...  51.4 us
    psum x2, blocking collectives, on_device(): sums = lax.psum(jnp.stack(sums), 'ga')  40.6 us
    dot_general x3, matrix products, project_occupied(): lax.dot_general(low_correlation, flat_panel, (((0,), (0,)), ((), ())), pr...  38.8 us
  transfers between devices with their start and end apart: 7, of which 5 were waited for; matrix products, arithmetic and copies ran while one was open for 21% of the time, Pallas kernels for 3%

profile of v1, /device:TPU:0, one launch (start us, length us, event | category | flops | bytes accessed | tf_op | source)
XLA Modules:
  0.0 915.5 jit_solution(12766400943675727818)
XLA Ops:
  11.1 9.4 %slice.133 = bf16[128,8,21,128]{3,2,1,0:T(8,128)(2,1)} slice(bf16[128,8,64,128]{3,2,1,0:T(8,128)(2,1)} %param.14), slice={[0:128], [0:8], [43:64], [0:128]} | slice | bytes 11010048 | tf_op jit(solution)/shard_map/slice | solution.py:73
  45.4 12.9 %fusion = bf16[128,43,8,128]{0,3,2,1:T(8,128)(2,1)} fusion(bf16[128,8,21,128]{0,3,1,2:T(8,128)(2,1)} %copy.122, bf16[128,8,22,128]{0,3,1,2:T(8,128)(2,1)} %copy.121, bf16[43,8,128]{2,1,0:T(8,128)(2,1)S(1)} %fusion.53), kind=kLoop, calls=%fused_computation.1 | loop fusion | flops 11272192 | bytes 22632448 | tf_op jit(solution)/shard_map/mul | solution.py:187
  60.1 38.2 %all_to_all.93 = bf16[8,43,8,128]{3,2,1,0:T(8,128)(2,1)S(1)} all-to-all(bf16[8,43,8,128]{3,2,1,0:T(8,128)(2,1)S(1)} %fusion.35), channel_id=1, replica_groups=mesh['ga'=8,'band'=2,'pool'=2] {'ga'}, dimensions={0} | all-to-all | bytes 1409024 | tf_op jit(solution)/shard_map/all_to_all | solution.py:174
  122.0 23.1 %grid_exact.1 = f32[3,43,64,128]{3,2,1,0:T(8,128)} custom-call(bf16[1,43,64,128]{3,2,1,0:T(8,128)(2,1)S(1)} %copy_bitcast_fusion.6.refs_0_, f32[3,64,64,128]{3,2,1,0:T(8,128)} %fusion.1.refs_1_, bf16[2,128,128]{2,1,0:T(8,128)(2,1)S(1)} %copy-done.1, bf16[2,64,128]{2,1,0:T(8,128)(2,1)S(1)} %copy-done.4, bf16[2,64,96]{2,1,0:T(8,128)(2,1)S(1)} %copy-done.3, ...), custom_call_target="tpu_custom_call" | custom-call | tf_op jit(solution)/shard_map/grid_exact/pallas_call | solution.py:125
  163.7 97.7 %all-to-all-done.1 = f32[3,43,64,128]{3,1,0,2:T(8,128)} async-done(((f32[3,43,64,128]{3,1,0,2:T(8,128)}), f32[3,43,64,128]{3,1,0,2:T(8,128)}, u32[]{:S(2)}, u32[]{:S(2)}) %all-to-all-start.1) | async-done | bytes 4227104 | tf_op jit(solution)/shard_map/all_to_all | solution.py:212
  280.6 82.5 %all-gather.3.cloned.1.call-done = bf16[256,44032]{0,1:T(8,128)(2,1)} async-done(((bf16[128,44032]{0,1:T(8,128)(2,1)}), bf16[256,44032]{0,1:T(8,128)(2,1)}) %all-gather.3.cloned.1.call-update) | async-done | bytes 22544400 | tf_op jit(solution)/shard_map/all_gather | solution.py:188
  363.0 12.7 %fusion.21 = f32[256,48]{0,1:T(8,128)S(1)} fusion(bf16[256,44032]{0,1:T(8,128)(2,1)} %all-gather.3.cloned.1.call-done, bf16[24,44032]{1,0:T(8,128)(2,1)} %bitcast.211, bf16[24,44032]{1,0:T(8,128)(2,1)} %multiply_convert_fusion), kind=kOutput, calls=%fused_computation.40 | convolution fusion | flops 1090584576 | bytes 26820608 | tf_op jit(solution)/shard_map/dot_general | solution.py:197
  375.7 37.8 %psum.35 = bf16[256,48]{0,1:T(8,128)(2,1)S(1)} all-reduce(f32[256,48]{0,1:T(8,128)S(1)} %fusion.21), channel_id=1, replica_groups=mesh['ga'=8,'band'=2,'pool'=2] {'ga'}, use_global_device_ids=true, to_apply=%region_0.1 | all-reduce | flops 12288 | bytes 73728 | tf_op jit(solution)/shard_map/psum | solution.py:200
  413.5 12.9 %fusion.67 = f32[48,44032]{1,0:T(8,128)} fusion(bf16[256,48]{0,1:T(8,128)(2,1)S(1)} %psum.35, bf16[256,44032]{0,1:T(8,128)(2,1)} %all-gather.3.cloned.1.call-done), kind=kOutput, calls=%fused_computation.136 | convolution fusion | flops 1082130432 | bytes 31023104 | tf_op jit(solution)/shard_map/dot_general | solution.py:202
  438.7 11.3 %fusion.60 = (bf16[24,43,8,128]{3,2,1,0:T(8,128)(2,1)}, f32[24,43,8,128]{3,2,1,0:T(8,128)}, f32[24,43,8,128]{3,2,1,0:T(8,128)}) fusion(f32[43,8,128]{2,1,0:T(8,128)S(1)} %get-tuple-element.47, f32[8,3,43,8,128]{4,3,2,1,0:T(8,128)} %copy.100, f32[24,43,8,128]{3,2,1,0:T(8,128)} %bitcast.207, f32[24,43,8,64]{3,2,1,0:T(8,128)} %get-tuple-element.39, ...), kind=kLoop, calls=%fused_computation.129 | loop fusion | flops 6340608 | bytes 23425024 | tf_op jit(solution)/shard_map/convert_element_type | solution.py:221
  467.1 29.5 %all-to-all-done.2 = bf16[24,43,8,128]{3,2,1,0:T(8,128)(2,1)} async-done(((bf16[24,43,8,128]{3,2,1,0:T(8,128)(2,1)}), bf16[24,43,8,128]{3,2,1,0:T(8,128)(2,1)}, u32[]{:S(2)}, u32[]{:S(2)}) %all-to-all-start.2) | async-done | bytes 2113568 | tf_op jit(solution)/shard_map/all_to_all | solution.py:174
  500.2 14.2 %grid_apply.2 = bf16[3,43,64,128]{3,2,1,0:T(8,128)(2,1)} custom-call(bf16[3,43,64,128]{3,2,1,0:T(8,128)(2,1)} %bitcast.216, f32[1,64,64,128]{3,2,1,0:T(8,128)S(1)} %pad_maximum_fusion.8.refs_1_, bf16[2,128,128]{2,1,0:T(8,128)(2,1)S(1)} %copy-done.1, bf16[2,64,128]{2,1,0:T(8,128)(2,1)S(1)} %copy-done.4, bf16[2,64,96]{2,1,0:T(8,128)(2,1)S(1)} %copy-done.3, ...), custom_call_target="tpu_custom_call" | custom-call | tf_op jit(solution)/shard_map/grid_apply/pallas_call | solution.py:125
  523.1 12.7 %fusion.25 = f32[256,48]{0,1:T(8,128)S(1)} fusion(bf16[256,44032]{0,1:T(8,128)(2,1)} %all-gather.3.cloned.1.call-done, bf16[24,44032]{1,0:T(8,128)(2,1)} %bitcast.210, bf16[24,44032]{1,0:T(8,128)(2,1)} %get-tuple-element.21), kind=kOutput, calls=%fused_computation.45 | convolution fusion | flops 1090584576 | bytes 26820608 | tf_op jit(solution)/shard_map/dot_general | solution.py:197
  535.8 61.8 %psum.36 = bf16[256,48]{0,1:T(8,128)(2,1)S(1)} all-reduce(f32[256,48]{0,1:T(8,128)S(1)} %fusion.25), channel_id=1, replica_groups=mesh['ga'=8,'band'=2,'pool'=2] {'ga'}, use_global_device_ids=true, to_apply=%region_1.2 | all-reduce | flops 12288 | bytes 73728 | tf_op jit(solution)/shard_map/psum | solution.py:200
  597.6 12.9 %fusion.66 = f32[48,44032]{1,0:T(8,128)} fusion(bf16[256,48]{0,1:T(8,128)(2,1)S(1)} %psum.36, bf16[256,44032]{0,1:T(8,128)(2,1)} %all-gather.3.cloned.1.call-done), kind=kOutput, calls=%fused_computation.135 | convolution fusion | flops 1082130432 | bytes 31023104 | tf_op jit(solution)/shard_map/dot_general | solution.py:202
  644.8 20.2 %psum.37 = f32[4,24]{1,0:T(4,128)S(1)} all-reduce(f32[4,24]{1,0:T(4,128)S(1)} %pad_maximum_fusion.10), channel_id=1, replica_groups=mesh['ga'=8,'band'=2,'pool'=2] {'ga'}, use_global_device_ids=true, to_apply=%region_5.6 | all-reduce | flops 96 | bytes 768 | tf_op jit(solution)/shard_map/psum | solution.py:238
  665.1 11.2 %fusion.34 = (bf16[24,43,8,128]{3,2,1,0:T(8,128)(2,1)}, f32[24,43,8,128]{3,2,1,0:T(8,128)}) fusion(f32[24,43,8,128]{3,2,1,0:T(8,128)} %get-tuple-element.24, f32[24]{0:T(128)S(1)} %get-tuple-element.17, f32[24,43,8,128]{3,2,1,0:T(8,128)} %bitcast.202, f32[43,8,128]{2,1,0:T(8,128)S(1)} %get-tuple-element.47, f32[8,3,43,8,128]{4,3,2,1,0:T(8,128)} %copy.105, ...), kind=kLoop, calls=%fused_computation.84 | loop fusion | flops 13737984 | bytes 23601440 | tf_op jit(solution)/shard_map/convert_element_type | solution.py:221
  690.1 29.7 %all-to-all-done.4 = bf16[24,43,8,128]{3,2,1,0:T(8,128)(2,1)} async-done(((bf16[24,43,8,128]{3,2,1,0:T(8,128)(2,1)}), bf16[24,43,8,128]{3,2,1,0:T(8,128)(2,1)}, u32[]{:S(2)}, u32[]{:S(2)}) %all-to-all-start.4) | async-done | bytes 2113568 | tf_op jit(solution)/shard_map/all_to_all | solution.py:174
  723.4 14.2 %grid_apply.3 = bf16[3,43,64,128]{3,2,1,0:T(8,128)(2,1)} custom-call(bf16[3,43,64,128]{3,2,1,0:T(8,128)(2,1)} %bitcast.212, f32[1,64,64,128]{3,2,1,0:T(8,128)S(1)} %pad_maximum_fusion.8.refs_1_, bf16[2,128,128]{2,1,0:T(8,128)(2,1)S(1)} %copy-done.1, bf16[2,64,128]{2,1,0:T(8,128)(2,1)S(1)} %copy-done.4, bf16[2,64,96]{2,1,0:T(8,128)(2,1)S(1)} %copy-done.3, ...), custom_call_target="tpu_custom_call" | custom-call | tf_op jit(solution)/shard_map/grid_apply/pallas_call | solution.py:125
  745.7 12.7 %fusion.29 = f32[256,48]{0,1:T(8,128)S(1)} fusion(bf16[256,44032]{0,1:T(8,128)(2,1)} %all-gather.3.cloned.1.call-done, bf16[24,44032]{1,0:T(8,128)(2,1)} %bitcast.209, bf16[24,44032]{1,0:T(8,128)(2,1)} %fusion.54), kind=kOutput, calls=%fused_computation.50 | convolution fusion | flops 1090584576 | bytes 26820608 | tf_op jit(solution)/shard_map/dot_general | solution.py:197
  758.3 62.1 %psum.38 = bf16[256,48]{0,1:T(8,128)(2,1)S(1)} all-reduce(f32[256,48]{0,1:T(8,128)S(1)} %fusion.29), channel_id=1, replica_groups=mesh['ga'=8,'band'=2,'pool'=2] {'ga'}, use_global_device_ids=true, to_apply=%region_6.7 | all-reduce | flops 12288 | bytes 73728 | tf_op jit(solution)/shard_map/psum | solution.py:200
  820.4 12.9 %fusion.65 = f32[48,44032]{1,0:T(8,128)} fusion(bf16[256,48]{0,1:T(8,128)(2,1)S(1)} %psum.38, bf16[256,44032]{0,1:T(8,128)(2,1)} %all-gather.3.cloned.1.call-done), kind=kOutput, calls=%fused_computation.134 | convolution fusion | flops 1082130432 | bytes 31023104 | tf_op jit(solution)/shard_map/dot_general | solution.py:202
  868.0 20.4 %psum.39 = f32[24]{0:T(128)S(1)} all-reduce(f32[24]{0:T(128)S(1)} %broadcast_multiply_fusion), channel_id=1, replica_groups=mesh['ga'=8,'band'=2,'pool'=2] {'ga'}, use_global_device_ids=true, to_apply=%region_8.9 | all-reduce | flops 24 | bytes 192 | tf_op jit(solution)/shard_map/psum | solution.py:238
  888.4 9.8 %fusion.16 = (f32[24,8,43,128]{3,1,2,0:T(8,128)S(1)}, f32[24,8,43,128]{3,1,2,0:T(8,128)S(1)}) fusion(f32[24,43,8,128]{3,2,1,0:T(8,128)} %get-tuple-element.16, f32[8,3,43,8,128]{4,3,2,1,0:T(8,128)} %copy.110, f32[24,43,8,128]{3,2,1,0:T(8,128)} %bitcast.201, f32[24]{0:T(128)S(1)} %div.75, f32[24]{0:T(128)S(1)} %sub.67, ...), kind=kLoop, calls=%fused_computation.26 | loop fusion | flops 15851520 | bytes 29942144 | tf_op jit(solution)/shard_map/transpose | solution.py:251
  (150 shorter events, 237.9 us)
Async XLA Ops:
  7.2 91.6 %all-gather.5.cloned.1.call-start = ((), (), s32[]{:S(2)}) async-start(), calls=%async_computation.7 | async-start | bytes 4718592 | tf_op jit(solution)/shard_map/all_gather | solution.py:181
  10.0 353.0 %all-gather.3.cloned.1.call-start = ((), (), s32[]{:S(2)}) async-start(), calls=%async_computation.6 | async-start | bytes 33816576 | tf_op jit(solution)/shard_map/all_gather | solution.py:188
  113.3 5.0 copy-start.6
  118.3 3.6 copy-start
  118.3 3.6 copy-start.1
  118.3 3.6 copy-start.2
  118.3 3.6 copy-start.3
  118.3 3.6 copy-start.4
  118.3 3.6 copy-start.5
  152.0 4.8 copy-start.15
  152.0 5.6 copy-start.13
  152.0 6.8 copy-start.17
  152.0 7.5 copy-start.16
  152.0 109.4 %all-to-all-start.1 = ((f32[3,43,64,128]{3,1,0,2:T(8,128)}), f32[3,43,64,128]{3,1,0,2:T(8,128)}, u32[]{:S(2)}, u32[]{:S(2)}) async-start(f32[3,43,64,128]{3,1,0,2:T(8,128)} %copy.98), calls=%async_computation.1 | async-start | bytes 9437184 | tf_op jit(solution)/shard_map/all_to_all | solution.py:212
  449.9 46.7 %all-to-all-start.2 = ((bf16[24,43,8,128]{3,2,1,0:T(8,128)(2,1)}), bf16[24,43,8,128]{3,2,1,0:T(8,128)(2,1)}, u32[]{:S(2)}, u32[]{:S(2)}) async-start(bf16[24,43,8,128]{3,2,1,0:T(8,128)(2,1)} %get-tuple-element.23), calls=%async_computation.2 | async-start | bytes 4227072 | tf_op jit(solution)/shard_map/all_to_all | solution.py:174
  454.7 8.8 copy-start.11
  518.8 107.1 %all-to-all-start.3 = ((bf16[3,43,64,128]{3,1,0,2:T(8,128)(2,1)}), bf16[3,43,64,128]{3,1,0,2:T(8,128)(2,1)}, u32[]{:S(2)}, u32[]{:S(2)}) async-start(bf16[3,43,64,128]{3,1,0,2:T(8,128)(2,1)} %copy.103), calls=%async_computation.3 | async-start | bytes 4718592 | tf_op jit(solution)/shard_map/all_to_all | solution.py:212
  619.4 3.3 copy-start.10
  676.2 43.6 %all-to-all-start.4 = ((bf16[24,43,8,128]{3,2,1,0:T(8,128)(2,1)}), bf16[24,43,8,128]{3,2,1,0:T(8,128)(2,1)}, u32[]{:S(2)}, u32[]{:S(2)}) async-start(bf16[24,43,8,128]{3,2,1,0:T(8,128)(2,1)} %get-tuple-element.15), calls=%async_computation.4 | async-start | bytes 4227072 | tf_op jit(solution)/shard_map/all_to_all | solution.py:174
  680.8 5.7 copy-start.12
  742.0 105.9 %all-to-all-start.5 = ((bf16[3,43,64,128]{3,1,0,2:T(8,128)(2,1)}), bf16[3,43,64,128]{3,1,0,2:T(8,128)(2,1)S(1)}, u32[]{:S(2)}, u32[]{:S(2)}) async-start(bf16[3,43,64,128]{3,1,0,2:T(8,128)(2,1)} %copy.108), calls=%async_computation.5 | async-start | bytes 4718592 | tf_op jit(solution)/shard_map/all_to_all | solution.py:212
  841.5 3.3 copy-start.8
  850.8 14.5 %slice-start.2 = ((s8[4227072]{0:T(1024)(128)(4,1)}), s8[32768]{0:T(1024)(128)(4,1)S(1)}, s32[]{:S(2)}) async-start(s8[4227072]{0:T(1024)(128)(4,1)} %bitcast.203), calls=%async_computation.10 | async-start | bytes 65536
  856.1 9.2 %slice-start.3 = ((s8[4227072]{0:T(1024)(128)(4,1)}), s8[4194304]{0:T(1024)(128)(4,1)S(1)}, s32[]{:S(2)}) async-start(s8[4227072]{0:T(1024)(128)(4,1)} %bitcast.203), calls=%async_computation.11 | async-start | bytes 8388608
  (5 other events, 10.3 us)
Sparse Core Ops, SparseCore 0:
  10.1 88.5 all-gather.4
  100.3 262.6 all-gather.2
